TPU v7x, 32 devices: a whole 2x2x4 slice. The times are simulated.
32 devices in a mesh: dev: 32 (over z, y, x, core).
Axes of the slice: x: 2, y: 2, z: 4, core: 2. Of those that a mesh axis runs over, the one named last changes fastest.
Arguments:
- rhs: float32 [135, 4096], P(None, 'dev')
- diag_blocks: bfloat16 [135, 135, 4096], P(None, None, 'dev')
- precond: bfloat16 [135, 135, 4096], P(None, None, 'dev')
- face_blocks: bfloat16 [6, 45, 45, 4096], P(None, None, None, 'dev'), may hold values from -0.4375 to 0.4375
- nbr_elem: int32 [6, 4096], P(None, 'dev'), may hold values from -1 to 4095, as said below
- nbr_face: int32 [6, 4096], P(None, 'dev'), may hold values from 0 to 5
- live: int32 [32], P('dev'), may hold values from 32 to 128, as said below
Outputs:
- basis: float32 [5, 135, 4096], P(None, None, 'dev')
- hessenberg: float32 [5, 4], replicated
- update: float32 [135, 4096], P(None, 'dev')
Inputs may be any that keep to these rules, and one draw needn't show every extreme that they name: `live`: some owner holds 128 elements and some owner holds 32. `nbr_elem`: A non-negative entry names a held element (slot below its owner's live count) whose owner is at most 2 positions away from the face's owner, counted cyclically over the owners; faces of empty slots hold -1. Faces of one owner name elements of any one other owner at most 48 times, and some owner reaches that.
All inputs are finite; a program needn't handle non-finite values.
Results may differ from a plain program's by a relative error of at most 0.025.
Values sent between devices are 32-bit elements; how exact they have to be, the bound alone decides.
A program may use at most 128 MiB of HBM per device.

v0:
```python
import jax
import jax.numpy as jnp
import numpy as np
from jax import lax
from jax.sharding import PartitionSpec as P

STEPS = 4


def from_behind(block, axis, distance):
    devices = range(lax.axis_size(axis))
    route = [((i - distance) % len(devices), i) for i in devices]
    return lax.ppermute(block, axis, route)


def face_table(variables):
    listing = []
    for face in range(6):
        direction = face // 2
        value = 0 if face % 2 == 0 else 2
        nodes = [
            node for node in range(27) if (node // 9, node // 3 % 3, node % 3)[direction] == value
        ]
        listing.append([var_index * 27 + node for var_index in range(variables) for node in nodes])
    return np.array(listing, dtype=np.int32)


def spread_table(variables):
    listing = face_table(variables)
    width = listing.shape[1]
    table = np.zeros((27 * variables, 6 * width), dtype=np.float32)
    for face in range(6):
        for entry in range(width):
            table[listing[face, entry], face * width + entry] = 1.0
    return table


def solve_small(matrix, vector):
    count = matrix.shape[0]
    for column in range(count):
        for row_index in range(column + 1, count):
            factor = matrix[row_index, column] / matrix[column, column]
            matrix = matrix.at[row_index].add(-factor * matrix[column])
            vector = vector.at[row_index].add(-factor * vector[column])
    result = [None] * count
    for row_index in range(count - 1, -1, -1):
        acc = vector[row_index]
        for column in range(row_index + 1, count):
            acc = acc - matrix[row_index, column] * result[column]
        result[row_index] = acc / matrix[row_index, row_index]
    return jnp.stack(result)


def per_device(rhs, diag_blocks, precond, face_blocks, nbr_elem, nbr_face, live):
    unknowns, slots = rhs.shape
    face_width = face_blocks.shape[1]
    variables = unknowns // 27
    owners = lax.axis_size("dev")
    position = lax.axis_index("dev")
    highest = lax.Precision.HIGHEST
    spread = jnp.asarray(spread_table(variables))
    trace_rows = jnp.asarray(face_table(variables))
    slot_ids = jnp.arange(slots, dtype=jnp.int32)
    live_mask = (slot_ids < live[0]).astype(jnp.float32)
    start = rhs * live_mask[None, :]
    scale = 1.0 / float(owners * slots * unknowns)
    targets = nbr_elem.reshape(-1)
    face_ids = nbr_face.reshape(-1)
    face_range = jnp.arange(6, dtype=jnp.int32)

    def deliver(values, goals, goal_faces):
        keep = (goals >= 0) & (goals // slots == position)
        local_slot = jnp.where(keep, goals % slots, -1)
        onehot_slot = (local_slot[:, None] == slot_ids[None, :]).astype(jnp.float32)
        onehot_face = (goal_faces[None, :] == face_range[:, None]).astype(jnp.float32)
        placed = (onehot_face[:, None, :] * values[None, :, :]).reshape(
            6 * face_width, values.shape[1]
        )
        summed = jnp.dot(placed, onehot_slot, precision=highest)
        return jnp.dot(spread, summed, precision=highest)

    beta = jnp.sqrt(lax.psum(jnp.sum(start * start), "dev") * scale + 1e-06)
    vectors = [start / beta]
    hessenberg = jnp.zeros((STEPS + 1, STEPS), jnp.float32)
    for step in range(STEPS):
        rounded = vectors[step].astype(jnp.bfloat16)
        applied = jnp.einsum(
            "ije,je->ie", precond, rounded, preferred_element_type=jnp.float32
        ).astype(jnp.bfloat16)
        own_part = jnp.einsum(
            "ije,je->ie", diag_blocks, applied, preferred_element_type=jnp.float32
        )
        traced = applied[trace_rows]
        contrib = jnp.einsum(
            "fkme,fme->kfe", face_blocks, traced, preferred_element_type=jnp.float32
        )
        contrib = contrib.reshape(face_width, 6 * slots)
        total = own_part + deliver(contrib, targets, face_ids)
        for offset in [1, -1, 2, -2]:
            operate_values, operate_goals, operate_goal_faces = from_behind(
                (contrib, targets, face_ids), "dev", offset
            )
            total = total + deliver(operate_values, operate_goals, operate_goal_faces)
        partial_dots = jnp.stack([jnp.sum(vec * total) for vec in vectors])
        summed_dots, summed_square = lax.psum((partial_dots, jnp.sum(total * total)), "dev")
        heights = summed_dots * scale
        rest = total
        for index in range(step + 1):
            rest = rest - heights[index] * vectors[index]
        height = jnp.sqrt(summed_square * scale - jnp.sum(heights * heights) + 1e-06)
        hessenberg = hessenberg.at[: step + 1, step].set(heights)
        hessenberg = hessenberg.at[step + 1, step].set(height)
        vectors.append(rest / height)
    gram = jnp.dot(hessenberg.T, hessenberg, precision=highest)
    coeffs = solve_small(gram, beta * hessenberg[0, :])
    combo = vectors[0] * coeffs[0]
    for index in range(1, STEPS):
        combo = combo + coeffs[index] * vectors[index]
    update = jnp.einsum(
        "ije,je->ie", precond, combo.astype(jnp.bfloat16), preferred_element_type=jnp.float32
    )
    return (jnp.stack(vectors), hessenberg, update)


def solution(mesh):
    in_specs = (
        P(None, "dev"),
        P(None, None, "dev"),
        P(None, None, "dev"),
        P(None, None, None, "dev"),
        P(None, "dev"),
        P(None, "dev"),
        P("dev"),
    )
    out_specs = (P(None, None, "dev"), P(), P(None, "dev"))
    return jax.shard_map(
        per_device, mesh=mesh, in_specs=in_specs, out_specs=out_specs, check_vma=False
    )
```

profile of v0, /device:TPU:12, one launch (start us, length us, event | category | flops | bytes accessed | tf_op | source)
XLA Modules:
  0.0 546.4 jit_solution(5767202196919265141)
XLA Ops:
  3.1 41.6 %psum.63 = f32[]{:T(128)} all-reduce(f32[]{:T(128)} %multiply_reduce_fusion.14), channel_id=1, replica_groups=mesh['dev'=32] {'dev'}, use_global_device_ids=true, to_apply=%region_1.0 | all-reduce | flops 1 | bytes 8 | tf_op jit(solution)/shard_map/psum | solution.py:82
  47.0 4.0 fusion.4
  56.3 2.6 collective-permute-start.4
  58.9 2.6 collective-permute-start.3
  75.0 4.0 fusion
  81.3 2.6 collective-permute-start.5
  84.7 3.9 collective-permute-done.6
  89.9 2.2 collective-permute-done.9
  92.2 3.4 collective-permute-start.7
  119.2 2.2 mul.607
  131.8 51.1 %all-reduce.4 = (f32[]{:T(128)}, f32[1]{0:T(128)}) all-reduce(f32[]{:T(128)} %get-tuple-element.256, f32[1]{0:T(128)} %bitcast.34), channel_id=1, replica_groups=mesh['dev'=32] {'dev'}, use_global_device_ids=true, to_apply=%region_5.6 | all-reduce | flops 2 | bytes 16 | tf_op jit(solution)/shard_map/psum | solution.py:105
  186.9 4.0 fusion.5
  192.1 2.4 gather_fusion.1
  201.2 2.6 collective-permute-start.13
  203.8 3.1 collective-permute-start.15
  211.5 4.0 fusion.1
  223.4 2.4 fusion.31
  229.9 2.4 fusion.27
  236.4 2.4 fusion.23
  248.6 2.6 multiply_reduce_fusion.11
  253.0 43.1 %all-reduce.3 = (f32[]{:T(128)}, f32[2]{0:T(128)}) all-reduce(f32[]{:T(128)} %get-tuple-element.253, f32[2]{0:T(128)} %pad_maximum_fusion), channel_id=1, replica_groups=mesh['dev'=32] {'dev'}, use_global_device_ids=true, to_apply=%region_10.11 | all-reduce | flops 3 | bytes 24 | tf_op jit(solution)/shard_map/psum | solution.py:105
  300.5 2.8 bitcast_convert_fusion.5
  303.4 4.0 fusion.6
  308.6 2.4 gather_fusion.2
  317.6 2.6 collective-permute-start.17
  320.7 2.9 collective-permute-start.19
  323.6 3.2 broadcast_select_fusion.2
  326.8 2.7 scatter.30
  329.5 2.2 mul.645
  333.4 4.0 fusion.2
  345.4 2.4 fusion.30
  351.9 2.4 fusion.26
  358.4 2.4 fusion.22
  370.5 2.6 multiply_reduce_fusion.8
  373.1 2.4 pad_maximum_fusion.1
  375.5 42.6 %all-reduce.2 = (f32[]{:T(128)}, f32[3]{0:T(128)}) all-reduce(f32[]{:T(128)} %get-tuple-element.249, f32[3]{0:T(128)} %pad_maximum_fusion.1), channel_id=1, replica_groups=mesh['dev'=32] {'dev'}, use_global_device_ids=true, to_apply=%region_17.18 | all-reduce | flops 4 | bytes 32 | tf_op jit(solution)/shard_map/psum | solution.py:105
  422.6 3.5 bitcast_convert_fusion.4
  426.1 4.0 fusion.7
  431.3 2.4 gather_fusion.3
  438.0 2.6 collective-permute-start.21
  440.6 2.9 collective-permute-start.23
  443.5 2.6 broadcast_select_fusion.1
  446.2 2.5 scatter.34
  449.5 4.0 fusion.3
  460.4 2.6 pad_maximum_fusion.2
  463.0 42.5 %all-reduce.1 = (f32[]{:T(128)}, f32[4]{0:T(128)S(1)}) all-reduce(f32[]{:T(128)} %get-tuple-element.244, f32[4]{0:T(128)S(1)} %pad_maximum_fusion.2), channel_id=1, replica_groups=mesh['dev'=32] {'dev'}, use_global_device_ids=true, to_apply=%region_25.26 | all-reduce | flops 5 | bytes 40 | tf_op jit(solution)/shard_map/psum | solution.py:105
  537.8 4.6 fusion.8
  543.0 3.1 bitcast_dynamic-update-slice_fusion
  (270 shorter events, 169.4 us)
Async XLA Ops:
  0.6 53.3 %copy-start.1 = (bf16[6,45,45,128]{3,2,1,0:T(8,128)(2,1)S(1)}, bf16[6,45,45,128]{3,2,1,0:T(8,128)(2,1)}, u32[]{:S(2)}) copy-start(bf16[6,45,45,128]{3,2,1,0:T(8,128)(2,1)} %param.52) | copy-start | bytes 9331204
  1.4 61.6 %copy-start.27 = (f32[128]{0:T(128)}, f32[128]{0:T(128)S(1)}, u32[]{:S(2)}) copy-start(f32[128]{0:T(128)S(1)} %compare_convert_fusion) | copy-start | bytes 1540
  47.0 11.9 %copy-start.32 = (s32[6,128]{1,0:T(8,128)S(1)}, s32[6,128]{1,0:T(8,128)}, u32[]{:S(2)}) copy-start(s32[6,128]{1,0:T(8,128)} %param.54) | copy-start | bytes 9220
  51.0 4.6 copy-start.2
  55.6 23.5 %copy-start = (f32[135,270]{1,0:T(8,128)S(1)}, f32[135,270]{1,0:T(8,128)}, u32[]{:S(2)}) copy-start(f32[135,270]{1,0:T(8,128)} %constant.638.clone) | copy-start | bytes 437404
  56.3 48.7 %collective-permute-start.1 = (f32[45,768]{1,0:T(8,128)}, f32[45,768]{1,0:T(8,128)}, u32[]{:S(2)}, u32[]{:S(2)}) collective-permute-start(f32[45,768]{1,0:T(8,128)} %bitcast.117), channel_id=1, source_target_pairs={{31,0},{0,1},{1,2},{2,3},{3,4},{4,5},{5,6},{6,7},{7,8},{8,9},{9,10... | collective-permute-start | bytes 414728 | tf_op jit(solution)/shard_map/ppermute | solution.py:13
  56.3 52.8 %collective-permute-start.4 = (f32[45,768]{1,0:T(8,128)}, f32[45,768]{1,0:T(8,128)}, u32[]{:S(2)}, u32[]{:S(2)}) collective-permute-start(f32[45,768]{1,0:T(8,128)} %bitcast.117), channel_id=1, source_target_pairs={{1,0},{2,1},{3,2},{4,3},{5,4},{6,5},{7,6},{8,7},{9,8},{10,9},{11,1... | collective-permute-start | bytes 414728 | tf_op jit(solution)/shard_map/ppermute | solution.py:13
  58.9 22.4 %collective-permute-start = (s32[768]{0:T(1024)S(1)}, s32[768]{0:T(1024)S(1)}, u32[]{:S(2)}, u32[]{:S(2)}) collective-permute-start(s32[768]{0:T(1024)S(1)} %bitcast.266), channel_id=1, source_target_pairs={{31,0},{0,1},{1,2},{2,3},{3,4},{4,5},{5,6},{6,7},{7,8},{8,9},{9,10... | collective-permute-start | bytes 9224 | tf_op jit(solution)/shard_map/ppermute | solution.py:13
  58.9 25.1 %collective-permute-start.3 = (s32[768]{0:T(1024)S(1)}, s32[768]{0:T(1024)S(1)}, u32[]{:S(2)}, u32[]{:S(2)}) collective-permute-start(s32[768]{0:T(1024)S(1)} %bitcast.267), channel_id=1, source_target_pairs={{1,0},{2,1},{3,2},{4,3},{5,4},{6,5},{7,6},{8,7},{9,8},{10,9},{11,1... | collective-permute-start | bytes 9224 | tf_op jit(solution)/shard_map/ppermute | solution.py:13
  61.6 34.0 %collective-permute-start.2 = (s32[768]{0:T(1024)}, s32[768]{0:T(1024)}, u32[]{:S(2)}, u32[]{:S(2)}) collective-permute-start(s32[768]{0:T(1024)} %bitcast.32), channel_id=1, source_target_pairs={{31,0},{0,1},{1,2},{2,3},{3,4},{4,5},{5,6},{6,7},{7,8},{8,9},{9,10... | collective-permute-start | bytes 9224 | tf_op jit(solution)/shard_map/ppermute | solution.py:13
  61.6 3.0 copy-start.13
  69.3 3.9 copy-start.21
  81.3 17.6 %collective-permute-start.5 = (s32[768]{0:T(1024)}, s32[768]{0:T(1024)S(1)}, u32[]{:S(2)}, u32[]{:S(2)}) collective-permute-start(s32[768]{0:T(1024)} %bitcast.32), channel_id=1, source_target_pairs={{1,0},{2,1},{3,2},{4,3},{5,4},{6,5},{7,6},{8,7},{9,8},{10,9},{11,1... | collective-permute-start | bytes 9224 | tf_op jit(solution)/shard_map/ppermute | solution.py:13
  84.0 21.1 %copy-start.18 = (f32[6,768]{1,0:T(8,128)}, f32[6,768]{1,0:T(8,128)S(1)}, u32[]{:S(2)}) copy-start(f32[6,768]{1,0:T(8,128)S(1)} %fusion.60) | copy-start | bytes 55300
  84.0 4.6 collective-permute-start.6
  88.5 3.6 collective-permute-start.9
  92.2 21.0 %collective-permute-start.7 = (f32[45,768]{1,0:T(8,128)}, f32[45,768]{1,0:T(8,128)}, u32[]{:S(2)}, u32[]{:S(2)}) collective-permute-start(f32[45,768]{1,0:T(8,128)} %bitcast.117), channel_id=1, source_target_pairs={{30,0},{31,1},{0,2},{1,3},{2,4},{3,5},{4,6},{5,7},{6,8},{7,9},{8,1... | collective-permute-start | bytes 414728 | tf_op jit(solution)/shard_map/ppermute | solution.py:13
  95.6 4.9 collective-permute-start.8
  98.9 18.3 %collective-permute-start.10 = (f32[45,768]{1,0:T(8,128)}, f32[45,768]{1,0:T(8,128)}, u32[]{:S(2)}, u32[]{:S(2)}) collective-permute-start(f32[45,768]{1,0:T(8,128)} %bitcast.117), channel_id=1, source_target_pairs={{2,0},{3,1},{4,2},{5,3},{6,4},{7,5},{8,6},{9,7},{10,8},{11,9},{12,... | collective-permute-start | bytes 414728 | tf_op jit(solution)/shard_map/ppermute | solution.py:13
  100.5 4.0 collective-permute-start.11
  121.4 7.4 %copy-start.10 = (f32[270,768]{1,0:T(8,128)S(1)}, f32[270,768]{1,0:T(8,128)}, u32[]{:S(2)}) copy-start(f32[270,768]{1,0:T(8,128)} %mul.607) | copy-start | bytes 2488324
  121.4 8.7 %copy-start.6 = (f32[135,128]{1,0:T(8,128)S(1)}, f32[135,128]{1,0:T(8,128)}, u32[]{:S(2)}) copy-start(f32[135,128]{1,0:T(8,128)} %param.49) | copy-start | bytes 207364
  121.4 8.7 %copy-start.28 = (f32[128]{0:T(128)S(1)}, f32[128]{0:T(128)}, u32[]{:S(2)}) copy-start(f32[128]{0:T(128)} %copy-done.27) | copy-start | bytes 1540
  196.0 3.2 copy-start.14
  201.2 18.1 %collective-permute-start.12 = (f32[45,768]{1,0:T(8,128)}, f32[45,768]{1,0:T(8,128)}, u32[]{:S(2)}, u32[]{:S(2)}) collective-permute-start(f32[45,768]{1,0:T(8,128)} %bitcast.120), channel_id=1, source_target_pairs={{31,0},{0,1},{1,2},{2,3},{3,4},{4,5},{5,6},{6,7},{7,8},{8,9},{9,10... | collective-permute-start | bytes 414728 | tf_op jit(solution)/shard_map/ppermute | solution.py:13
  201.2 24.7 %collective-permute-start.13 = (f32[45,768]{1,0:T(8,128)}, f32[45,768]{1,0:T(8,128)}, u32[]{:S(2)}, u32[]{:S(2)}) collective-permute-start(f32[45,768]{1,0:T(8,128)} %bitcast.120), channel_id=1, source_target_pairs={{1,0},{2,1},{3,2},{4,3},{5,4},{6,5},{7,6},{8,7},{9,8},{10,9},{11,1... | collective-permute-start | bytes 414728 | tf_op jit(solution)/shard_map/ppermute | solution.py:13
  203.8 28.5 %collective-permute-start.14 = (f32[45,768]{1,0:T(8,128)}, f32[45,768]{1,0:T(8,128)}, u32[]{:S(2)}, u32[]{:S(2)}) collective-permute-start(f32[45,768]{1,0:T(8,128)} %bitcast.120), channel_id=1, source_target_pairs={{30,0},{31,1},{0,2},{1,3},{2,4},{3,5},{4,6},{5,7},{6,8},{7,9},{8,1... | collective-permute-start | bytes 414728 | tf_op jit(solution)/shard_map/ppermute | solution.py:13
  203.8 35.0 %collective-permute-start.15 = (f32[45,768]{1,0:T(8,128)}, f32[45,768]{1,0:T(8,128)}, u32[]{:S(2)}, u32[]{:S(2)}) collective-permute-start(f32[45,768]{1,0:T(8,128)} %bitcast.120), channel_id=1, source_target_pairs={{2,0},{3,1},{4,2},{5,3},{6,4},{7,5},{8,6},{9,7},{10,8},{11,9},{12,... | collective-permute-start | bytes 414728 | tf_op jit(solution)/shard_map/ppermute | solution.py:13
  312.5 3.2 copy-start.15
  312.5 11.1 %copy-start.34 = (f32[2]{0:T(128)S(1)}, f32[2]{0:T(128)}, u32[]{:S(2)}) copy-start(f32[2]{0:T(128)} %get-tuple-element.262) | copy-start | bytes 28
  317.6 23.7 %collective-permute-start.16 = (f32[45,768]{1,0:T(8,128)}, f32[45,768]{1,0:T(8,128)}, u32[]{:S(2)}, u32[]{:S(2)}) collective-permute-start(f32[45,768]{1,0:T(8,128)} %bitcast.123), channel_id=1, source_target_pairs={{31,0},{0,1},{1,2},{2,3},{3,4},{4,5},{5,6},{6,7},{7,8},{8,9},{9,10... | collective-permute-start | bytes 414728 | tf_op jit(solution)/shard_map/ppermute | solution.py:13
  317.6 30.2 %collective-permute-start.17 = (f32[45,768]{1,0:T(8,128)}, f32[45,768]{1,0:T(8,128)}, u32[]{:S(2)}, u32[]{:S(2)}) collective-permute-start(f32[45,768]{1,0:T(8,128)} %bitcast.123), channel_id=1, source_target_pairs={{1,0},{2,1},{3,2},{4,3},{5,4},{6,5},{7,6},{8,7},{9,8},{10,9},{11,1... | collective-permute-start | bytes 414728 | tf_op jit(solution)/shard_map/ppermute | solution.py:13
  320.3 34.0 %collective-permute-start.18 = (f32[45,768]{1,0:T(8,128)}, f32[45,768]{1,0:T(8,128)}, u32[]{:S(2)}, u32[]{:S(2)}) collective-permute-start(f32[45,768]{1,0:T(8,128)} %bitcast.123), channel_id=1, source_target_pairs={{30,0},{31,1},{0,2},{1,3},{2,4},{3,5},{4,6},{5,7},{6,8},{7,9},{8,1... | collective-permute-start | bytes 414728 | tf_op jit(solution)/shard_map/ppermute | solution.py:13
  320.7 40.1 %collective-permute-start.19 = (f32[45,768]{1,0:T(8,128)}, f32[45,768]{1,0:T(8,128)}, u32[]{:S(2)}, u32[]{:S(2)}) collective-permute-start(f32[45,768]{1,0:T(8,128)} %bitcast.123), channel_id=1, source_target_pairs={{2,0},{3,1},{4,2},{5,3},{6,4},{7,5},{8,6},{9,7},{10,8},{11,9},{12,... | collective-permute-start | bytes 414728 | tf_op jit(solution)/shard_map/ppermute | solution.py:13
  433.7 15.2 %copy-start.22 = (s32[768]{0:T(1024)S(1)}, s32[768]{0:T(1024)}, u32[]{:S(2)}) copy-start(s32[768]{0:T(1024)} %copy-done.21) | copy-start | bytes 9220
  435.2 8.3 %copy-start.33 = (f32[3]{0:T(128)S(1)}, f32[3]{0:T(128)}, u32[]{:S(2)}) copy-start(f32[3]{0:T(128)} %get-tuple-element.260) | copy-start | bytes 40
  437.7 11.8 %copy-start.20 = (f32[128,135]{0,1:T(8,128)S(1)}, f32[128,135]{0,1:T(8,128)}, u32[]{:S(2)}) copy-start(f32[128,135]{0,1:T(8,128)} %convert.91) | copy-start | bytes 207364
  437.8 16.4 %copy-start.11 = (f32[135,128]{1,0:T(8,128)S(1)}, f32[135,128]{1,0:T(8,128)}, u32[]{:S(2)}) copy-start(f32[135,128]{1,0:T(8,128)} %get-tuple-element.268) | copy-start | bytes 207364
  437.8 17.0 %copy-start.19 = (f32[6,768]{1,0:T(8,128)S(1)}, f32[6,768]{1,0:T(8,128)}, u32[]{:S(2)}) copy-start(f32[6,768]{1,0:T(8,128)} %copy-done.18) | copy-start | bytes 55300
  437.9 16.9 %collective-permute-start.20 = (f32[45,768]{1,0:T(8,128)S(1)}, f32[45,768]{1,0:T(8,128)S(1)}, u32[]{:S(2)}, u32[]{:S(2)}) collective-permute-start(f32[45,768]{1,0:T(8,128)S(1)} %bitcast.260), channel_id=1, source_target_pairs={{31,0},{0,1},{1,2},{2,3},{3,4},{4,5},{5,6},{6,7},{7,8},{8,9},{9,10... | collective-permute-start | bytes 414728 | tf_op jit(solution)/shard_map/ppermute | solution.py:13
  438.0 17.7 %collective-permute-start.21 = (f32[45,768]{1,0:T(8,128)S(1)}, f32[45,768]{1,0:T(8,128)S(1)}, u32[]{:S(2)}, u32[]{:S(2)}) collective-permute-start(f32[45,768]{1,0:T(8,128)S(1)} %bitcast.261), channel_id=1, source_target_pairs={{1,0},{2,1},{3,2},{4,3},{5,4},{6,5},{7,6},{8,7},{9,8},{10,9},{11,1... | collective-permute-start | bytes 414728 | tf_op jit(solution)/shard_map/ppermute | solution.py:13
  440.6 16.0 %collective-permute-start.22 = (f32[45,768]{1,0:T(8,128)S(1)}, f32[45,768]{1,0:T(8,128)S(1)}, u32[]{:S(2)}, u32[]{:S(2)}) collective-permute-start(f32[45,768]{1,0:T(8,128)S(1)} %bitcast.262), channel_id=1, source_target_pairs={{30,0},{31,1},{0,2},{1,3},{2,4},{3,5},{4,6},{5,7},{6,8},{7,9},{8,1... | collective-permute-start | bytes 414728 | tf_op jit(solution)/shard_map/ppermute | solution.py:13
  440.6 16.8 %collective-permute-start.23 = (f32[45,768]{1,0:T(8,128)S(1)}, f32[45,768]{1,0:T(8,128)S(1)}, u32[]{:S(2)}, u32[]{:S(2)}) collective-permute-start(f32[45,768]{1,0:T(8,128)S(1)} %bitcast.263), channel_id=1, source_target_pairs={{2,0},{3,1},{4,2},{5,3},{6,4},{7,5},{8,6},{9,7},{10,8},{11,9},{12,... | collective-permute-start | bytes 414728 | tf_op jit(solution)/shard_map/ppermute | solution.py:13
  448.7 5.1 copy-start.30
  448.9 6.2 %copy-start.26 = (s32[768]{0:T(1024)S(1)}, s32[768]{0:T(1024)}, u32[]{:S(2)}) copy-start(s32[768]{0:T(1024)} %fusion.67) | copy-start | bytes 9220
  449.5 6.2 %copy-start.17 = (f32[6,768]{1,0:T(8,128)S(1)}, f32[6,768]{1,0:T(8,128)}, u32[]{:S(2)}) copy-start(f32[6,768]{1,0:T(8,128)} %fusion.61) | copy-start | bytes 55300
  453.5 3.1 copy-start.12
  511.1 35.1 %copy-start.31 = (f32[5,4]{0,1:T(4,128)}, f32[5,4]{0,1:T(4,128)S(1)}, u32[]{:S(2)}) copy-start(f32[5,4]{0,1:T(4,128)S(1)} %scatter.39) | copy-start | bytes 244
  (11 other events, 21.8 us)
where the time goes:
time: 557 us; the launch traced here: 546 us
  blocking collectives  221 us (40%)
  other arithmetic  123 us (22%)
  local copies, waits for them, and re-layouts  76.8 us (14%)
  matrix products  55.1 us (10%)
  starting transfers between devices  34.1 us (6%)
  between operations  28.8 us (5%)
  waiting for transfers between devices  8 us (1%)
    psum x4, blocking collectives, per_device(): lax.psum((partial_dots, jnp.sum(total * total)), 'dev')  179 us
    psum x1, blocking collectives, per_device(): beta = jnp.sqrt(lax.psum(jnp.sum(start * start), 'dev') * scale + 1e-06)  41.6 us
    ppermute x24, starting transfers between devices, from_behind(): return lax.ppermute(block, axis, route)  34.1 us
    mul x20, local copies, waits for them, and re-layouts, deliver(): onehot_face[:, None, :] * values[None, :, :]  33.2 us
    dot_general x20, matrix products, deliver(): summed = jnp.dot(placed, onehot_slot, precision=highest)  32.9 us
    mul x20, other arithmetic, deliver(): onehot_face[:, None, :] * values[None, :, :]  29 us
    unnamed x18, other arithmetic  23.5 us
    dot_general x20, matrix products, deliver(): return jnp.dot(spread, summed, precision=highest)  22 us
  transfers between devices with their start and end apart: 24, of which 3 were waited for; matrix products, arithmetic and copies ran while one was open for 22% of the time, Pallas kernels for 0%

commit v1 on v0

v1 whole, which is shorter than its diff:
```python
import functools

import jax
import jax.numpy as jnp
import numpy as np
from jax import lax
from jax.experimental import pallas as pl
from jax.experimental.pallas import tpu as pltpu
from jax.sharding import PartitionSpec as P

STEPS = 4
NODES = 27
FACES = 6
OFFSETS = (1, -1, 2, -2)
MESH = pl.DeviceIdType.MESH


def face_table(variables):
    listing = []
    for face in range(FACES):
        direction = face // 2
        value = 0 if face % 2 == 0 else 2
        nodes = [
            node
            for node in range(NODES)
            if (node // 9, node // 3 % 3, node % 3)[direction] == value
        ]
        listing.append([v * NODES + node for v in range(variables) for node in nodes])
    return np.array(listing, dtype=np.int32)


def spread_table(variables, pitch):
    listing = face_table(variables)
    table = np.zeros((NODES * variables, FACES * pitch), dtype=np.float32)
    for face in range(FACES):
        for entry in range(listing.shape[1]):
            table[listing[face, entry], face * pitch + entry] = 1.0
    return table


def row_sums(block, vector, split):
    half = split // 2
    head = block[:, :half] * vector[None, :half] + block[:, half:split] * vector[None, half:split]
    tail = block[:, split:] * vector[None, split:]
    both = jnp.concatenate([head.astype(jnp.float32), tail.astype(jnp.float32)], axis=1)
    return jnp.sum(both, axis=1)


def kernel(
    owners, live_ref, rhs_ref, nbr_elem_ref, nbr_face_ref, spread_ref, trace_ref,
    diag_hbm, precond_hbm, face_hbm,
    basis_ref, hess_ref, update_ref,
    diag, precond, face, image, fields, contrib, local_place, send_place,
    halo_out, halo_in, dots_out, dots_in,
    load_sems, halo_send, halo_recv, dots_send, dots_recv,
):
    f32, bf16 = jnp.float32, jnp.bfloat16
    unknowns, slots = rhs_ref.shape
    width = face.shape[1]
    pitch = contrib.shape[0]
    lanes = FACES * slots
    me = lax.axis_index("dev")
    scale = 1.0 / float(owners * slots * unknowns)

    loads = [
        pltpu.make_async_copy(src, dst, load_sems.at[k])
        for k, (src, dst) in enumerate(
            [(precond_hbm, precond), (face_hbm, face), (diag_hbm, diag)]
        )
    ]
    for load in loads:
        load.start()

    barrier = pltpu.get_barrier_semaphore()

    def greet(k, carry):
        pl.semaphore_signal(
            barrier, inc=1, device_id=(lax.rem(me + k, owners),), device_id_type=MESH
        )
        return carry

    lax.fori_loop(1, owners, greet, 0)

    live_mask = (lax.broadcasted_iota(jnp.int32, (1, slots), 1) < live_ref[0]).astype(f32)
    start = rhs_ref[...] * live_mask
    on_diag = lax.broadcasted_iota(jnp.int32, (8, 128), 0) == lax.broadcasted_iota(
        jnp.int32, (8, 128), 1
    )

    def begin_total(round_id, rows):
        rows = rows + [jnp.zeros((8 - len(rows), slots), f32)]
        sums = jnp.sum(jnp.concatenate(rows, axis=0), axis=1, keepdims=True)
        mine = jnp.sum(jnp.where(on_diag, sums, 0.0), axis=0, keepdims=True)
        dots_out[round_id] = mine

        def push(k, carry):
            pltpu.make_async_remote_copy(
                src_ref=dots_out.at[round_id],
                dst_ref=dots_in.at[round_id, k - 1],
                send_sem=dots_send.at[round_id],
                recv_sem=dots_recv.at[round_id],
                device_id=(lax.rem(me + k, owners),),
                device_id_type=MESH,
            ).start()
            return carry

        lax.fori_loop(1, owners, push, 0)
        return mine

    def end_total(round_id, mine):
        arrived = dots_in.at[round_id]
        pltpu.make_async_copy(arrived, arrived, dots_recv.at[round_id]).wait()
        return mine + jnp.sum(dots_in[round_id], axis=0)

    first = [jnp.sum(start * start, axis=0, keepdims=True)]
    pl.semaphore_wait(barrier, owners - 1)
    mine = begin_total(0, first)

    goals = nbr_elem_ref[...]
    goal_face = nbr_face_ref[...]
    goal_owner = goals // slots
    goal_slot = goals % slots
    held = goals >= 0
    sub = lax.broadcasted_iota(jnp.int32, (slots, slots), 0)
    lane = lax.broadcasted_iota(jnp.int32, (slots, slots), 1)
    own = held & (goal_owner == me)
    own_slot = jnp.where(own, goal_slot, -1)
    upto = (sub <= lane).astype(bf16)
    every = jnp.ones((slots, slots), bf16)
    keeps = [
        held & (goal_owner == lax.rem(me + offset + owners, owners)) for offset in OFFSETS
    ]
    before = (
        lax.broadcasted_iota(jnp.int32, (FACES, FACES), 1)
        < lax.broadcasted_iota(jnp.int32, (FACES, FACES), 0)
    ).astype(f32)
    for f in range(FACES):
        local_place[:, f * slots : (f + 1) * slots] = (sub == own_slot[f : f + 1]).astype(
            f32
        ).astype(bf16)
    for d, keep in enumerate(keeps):
        mask = keep.astype(f32).astype(bf16)
        within = jnp.dot(mask, upto, preferred_element_type=f32)
        totals = jnp.dot(mask, every, preferred_element_type=f32)
        earlier = jnp.dot(
            before, totals, preferred_element_type=f32, precision=lax.Precision.HIGHEST
        )
        rank = jnp.where(keep, (within + earlier).astype(jnp.int32) - 1, -1)
        for f in range(FACES):
            send_place[d * 128 : (d + 1) * 128, f * slots : (f + 1) * slots] = (
                sub == rank[f : f + 1]
            ).astype(f32).astype(bf16)
    for f in range(FACES):
        at = slice(f * slots, (f + 1) * slots)
        contrib[width : width + 1, at] = goal_slot[f : f + 1].astype(f32)
        contrib[width + 1 : width + 2, at] = goal_face[f : f + 1].astype(f32) + 1.0
        contrib[width + 2 : pitch, at] = jnp.zeros((pitch - width - 2, slots), f32)
    face_row = jnp.concatenate([goal_face[f : f + 1] for f in range(FACES)], axis=1)

    def by_lane(row, index):
        return row[:, index : index + 1]

    norm = by_lane(end_total(0, mine), 0) * scale
    beta = jnp.sqrt(norm + 1e-06)
    basis_ref[0] = start / beta
    cross = {(0, 0): norm / (beta * beta)}
    hess = {}
    arrived_place = None

    for step in range(STEPS):
        rounded = basis_ref[step].astype(bf16)
        if step == 0:
            loads[0].wait()

        def precondition(b, carry):
            at = pl.ds(pl.multiple_of(b * 8, 8), 8)
            fields[step, at, :] = row_sums(precond[at], rounded, 128)
            return carry

        whole = unknowns // 8
        lax.fori_loop(0, whole, precondition, 0)
        fields[step, whole * 8 : unknowns, :] = row_sums(
            precond[whole * 8 : unknowns], rounded, 128
        )
        applied = fields[step, :unknowns, :].astype(bf16)
        traced = jnp.dot(trace_ref[...], applied, preferred_element_type=f32).astype(bf16)
        if step == 0:
            loads[1].wait()
        for f in range(FACES):
            vector = traced[f * pitch : f * pitch + width]
            at = slice(f * slots, (f + 1) * slots)
            for k in range(0, width, 8):
                top = min(k + 8, width)
                contrib[k:top, at] = row_sums(face[f, k:top], vector, 32)
        sent = contrib[...].astype(bf16)
        packed = lax.dot_general(
            sent, send_place[...], (((1,), (1,)), ((), ())), preferred_element_type=f32
        )
        for d in range(len(OFFSETS)):
            halo_out[step, d] = packed[:, d * 128 : (d + 1) * 128]
        copies = []
        for d, offset in enumerate(OFFSETS):
            copies.append(
                pltpu.make_async_remote_copy(
                    src_ref=halo_out.at[step, d],
                    dst_ref=halo_in.at[step, d],
                    send_sem=halo_send.at[step, d],
                    recv_sem=halo_recv.at[step, d],
                    device_id=(lax.rem(me + offset + owners, owners),),
                    device_id_type=MESH,
                )
            )
            copies[-1].start()

        if step == 0:
            loads[2].wait()

        def diagonal(b, carry):
            at = pl.ds(pl.multiple_of(b * 8, 8), 8)
            image[at, :] = row_sums(diag[at], applied, 128)
            return carry

        lax.fori_loop(0, whole, diagonal, 0)
        image[whole * 8 : unknowns, :] = row_sums(diag[whole * 8 : unknowns], applied, 128)

        def deliver(values, faces_at, place, shift):
            placed = jnp.concatenate(
                [jnp.where(faces_at == g + shift, values, 0.0) for g in range(FACES)], axis=0
            ).astype(bf16)
            return lax.dot_general(
                placed, place, (((1,), (1,)), ((), ())), preferred_element_type=f32
            )

        at_faces = deliver(contrib[...], face_row, local_place[...], 0)
        for copy in copies:
            copy.wait_recv()
        got = jnp.concatenate([halo_in[step, d] for d in range(len(OFFSETS))], axis=1)
        got_slot = got[width : width + 1].astype(jnp.int32)
        got_face = got[width + 1 : width + 2].astype(jnp.int32)
        if step == 0:
            spots = lax.broadcasted_iota(jnp.int32, (slots, got.shape[1]), 0)
            arrived_place = (spots == got_slot).astype(f32).astype(bf16)
        at_faces = at_faces + deliver(got, got_face, arrived_place, 1)
        total = image[:unknowns, :] + jnp.dot(
            spread_ref[...], at_faces.astype(bf16), preferred_element_type=f32
        )
        vectors = [basis_ref[i] for i in range(step + 1)]
        mine = begin_total(
            step + 1,
            [jnp.sum(v * total, axis=0, keepdims=True) for v in vectors]
            + [jnp.sum(total * total, axis=0, keepdims=True)],
        )
        summed = end_total(step + 1, mine) * scale
        heights = [by_lane(summed, i) for i in range(step + 1)]
        rest = total
        for h, v in zip(heights, vectors):
            rest = rest - h * v
        along = [
            heights[i]
            - sum(heights[k] * cross[min(i, k), max(i, k)] for k in range(step + 1))
            for i in range(step + 1)
        ]
        square = by_lane(summed, step + 1) - sum(
            heights[i] * (heights[i] + along[i]) for i in range(step + 1)
        )
        square = jnp.maximum(square, 0.0)
        height = jnp.sqrt(square + 1e-06)
        inverse = 1.0 / height
        basis_ref[step + 1] = rest * inverse
        for i in range(step + 1):
            hess[i, step] = heights[i]
            cross[i, step + 1] = along[i] * inverse
        hess[step + 1, step] = height
        cross[step + 1, step + 1] = square * inverse * inverse

    rows = lax.broadcasted_iota(jnp.int32, hess_ref.shape, 0)
    cols = lax.broadcasted_iota(jnp.int32, hess_ref.shape, 1)
    table = jnp.zeros(hess_ref.shape, f32)
    for (i, j), value in hess.items():
        table = jnp.where((rows == i) & (cols == j), value, table)
    hess_ref[...] = table

    matrix = [
        [
            sum(hess[r, i] * hess[r, j] for r in range(min(i, j) + 2))
            for j in range(STEPS)
        ]
        for i in range(STEPS)
    ]
    vector = [beta * hess[0, j] for j in range(STEPS)]
    for c in range(STEPS):
        pivot = 1.0 / matrix[c][c]
        for r in range(c + 1, STEPS):
            factor = matrix[r][c] * pivot
            for k in range(c, STEPS):
                matrix[r][k] = matrix[r][k] - factor * matrix[c][k]
            vector[r] = vector[r] - factor * vector[c]
    coeffs = [None] * STEPS
    for r in range(STEPS - 1, -1, -1):
        acc = vector[r]
        for k in range(r + 1, STEPS):
            acc = acc - matrix[r][k] * coeffs[k]
        coeffs[r] = acc / matrix[r][r]
    update = coeffs[0] * fields[0, :unknowns, :]
    for i in range(1, STEPS):
        update = update + coeffs[i] * fields[i, :unknowns, :]
    update_ref[...] = update

    for step in range(STEPS):
        for d in range(len(OFFSETS)):
            out = halo_out.at[step, d]
            pltpu.make_async_copy(out, out, halo_send.at[step, d]).wait()
    for round_id in range(STEPS + 1):
        arrived = dots_in.at[round_id]
        pltpu.make_async_copy(arrived, arrived, dots_send.at[round_id]).wait()


def per_device(rhs, diag_blocks, precond, face_blocks, nbr_elem, nbr_face, live):
    unknowns, slots = rhs.shape
    width = face_blocks.shape[1]
    owners = lax.axis_size("dev")
    variables = unknowns // NODES
    pitch = (width + 2 + 7) // 8 * 8
    padded = (unknowns + 7) // 8 * 8
    table = spread_table(variables, pitch)
    spread = jnp.asarray(table, jnp.bfloat16)
    trace = jnp.asarray(table.T, jnp.bfloat16)
    f32, bf16 = jnp.float32, jnp.bfloat16
    vmem = pl.BlockSpec(memory_space=pltpu.VMEM)
    smem = pl.BlockSpec(memory_space=pltpu.SMEM)
    hbm = pl.BlockSpec(memory_space=pl.ANY)
    sides = len(OFFSETS)
    dma = pltpu.SemaphoreType.DMA
    return pl.pallas_call(
        functools.partial(kernel, owners),
        out_shape=(
            jax.ShapeDtypeStruct((STEPS + 1, unknowns, slots), f32),
            jax.ShapeDtypeStruct((STEPS + 1, STEPS), f32),
            jax.ShapeDtypeStruct((unknowns, slots), f32),
        ),
        in_specs=[smem, vmem, vmem, vmem, vmem, vmem, hbm, hbm, hbm],
        out_specs=(vmem, vmem, vmem),
        scratch_shapes=[
            pltpu.VMEM(diag_blocks.shape, bf16),
            pltpu.VMEM(precond.shape, bf16),
            pltpu.VMEM(face_blocks.shape, bf16),
            pltpu.VMEM((padded, slots), f32),
            pltpu.VMEM((STEPS, padded, slots), f32),
            pltpu.VMEM((pitch, FACES * slots), f32),
            pltpu.VMEM((slots, FACES * slots), bf16),
            pltpu.VMEM((sides * 128, FACES * slots), bf16),
            pltpu.VMEM((STEPS, sides, pitch, 128), f32),
            pltpu.VMEM((STEPS, sides, pitch, 128), f32),
            pltpu.VMEM((STEPS + 1, 1, 128), f32),
            pltpu.VMEM((STEPS + 1, owners - 1, 1, 128), f32),
            dma((3,)),
            dma((STEPS, sides)),
            dma((STEPS, sides)),
            dma((STEPS + 1,)),
            dma((STEPS + 1,)),
        ],
        compiler_params=pltpu.CompilerParams(
            collective_id=0, has_side_effects=True, vmem_limit_bytes=56 * 1024 * 1024
        ),
    )(live, rhs, nbr_elem, nbr_face, spread, trace, diag_blocks, precond, face_blocks)


def solution(mesh):
    in_specs = (
        P(None, "dev"),
        P(None, None, "dev"),
        P(None, None, "dev"),
        P(None, None, None, "dev"),
        P(None, "dev"),
        P(None, "dev"),
        P("dev"),
    )
    out_specs = (P(None, None, "dev"), P(), P(None, "dev"))
    return jax.shard_map(
        per_device, mesh=mesh, in_specs=in_specs, out_specs=out_specs, check_vma=False
    )
```

time: 557 us -> 70 us (0.13)
  the two profiles are of different devices: /device:TPU:12 before, /device:TPU:0 now
where the time goes in v1:
time: 70 us; the launch traced here: 69.8 us
  Pallas kernels  63.9 us (91%)
  local copies, waits for them, and re-layouts  4.58 us (7%)
  between operations  1.29 us (2%)
    pallas_call x1, Pallas kernels, per_device(): pl.pallas_call(functools.partial(kernel, owners), out_shape=(jax.ShapeDty...  63.9 us
    unnamed x2, local copies, waits for them, and re-layouts  3.25 us

profile of v1, /device:TPU:0, one launch (start us, length us, event | category | flops | bytes accessed | tf_op | source)
XLA Modules:
  0.0 69.8 jit_solution(1291965893904702513)
XLA Ops:
  1.3 63.9 %shard_map.112 = (f32[5,135,128]{2,1,0:T(8,128)}, f32[5,4]{1,0:T(8,128)}, f32[135,128]{1,0:T(8,128)}) custom-call(s32[1]{0:T(128)S(6)} %copy.15.live_ref, f32[135,128]{1,0:T(8,128)} %rhs_ref.1, s32[6,128]{1,0:T(8,128)} %nbr_elem_ref.1, s32[6,128]{1,0:T(8,128)} %nbr_face_ref.1, bf16[135,288]{1,0:T(8,128)(2,1)} %constant.4.clone.spread_ref, ...), custom_call_target="tpu_custom_call" | custom-call | tf_op jit(solution)/shard_map/pallas_call | solution.py:334
  65.2 1.3 %copy.12 = f32[5,4]{0,1:T(4,128)} copy(f32[5,4]{1,0:T(8,128)} %get-tuple-element.4) | data formatting | bytes 160 | tf_op jit(solution)/shard_map/pallas_call | solution.py:334
  66.5 1.7 %copy.16 = f32[5,135,128]{2,1,0:T(8,128)} copy(f32[5,135,128]{2,1,0:T(8,128)} %get-tuple-element.9) | data formatting | bytes 691200
  68.3 1.5 %copy.17 = f32[135,128]{1,0:T(8,128)} copy(f32[135,128]{1,0:T(8,128)} %get-tuple-element.11) | data formatting | bytes 138240

commit v2 on v1

--- a/solution.py
+++ b/solution.py
@@ -50,7 +50,7 @@
     owners, live_ref, rhs_ref, nbr_elem_ref, nbr_face_ref, spread_ref, trace_ref,
     diag_hbm, precond_hbm, face_hbm,
     basis_ref, hess_ref, update_ref,
-    diag, precond, face, image, fields, contrib, local_place, send_place,
+    diag, precond, face, images, fields, contrib, local_place, send_place,
     halo_out, halo_in, dots_out, dots_in,
     load_sems, halo_send, halo_recv, dots_send, dots_recv,
 ):
@@ -58,7 +58,8 @@
     unknowns, slots = rhs_ref.shape
     width = face.shape[1]
     pitch = contrib.shape[0]
-    lanes = FACES * slots
+    room = slots // 2
+    half = pitch // 2
     me = lax.axis_index("dev")
     scale = 1.0 / float(owners * slots * unknowns)
 
@@ -111,10 +112,6 @@
         arrived = dots_in.at[round_id]
         pltpu.make_async_copy(arrived, arrived, dots_recv.at[round_id]).wait()
         return mine + jnp.sum(dots_in[round_id], axis=0)
-
-    first = [jnp.sum(start * start, axis=0, keepdims=True)]
-    pl.semaphore_wait(barrier, owners - 1)
-    mine = begin_total(0, first)
 
     goals = nbr_elem_ref[...]
     goal_face = nbr_face_ref[...]
@@ -147,28 +144,86 @@
         )
         rank = jnp.where(keep, (within + earlier).astype(jnp.int32) - 1, -1)
         for f in range(FACES):
-            send_place[d * 128 : (d + 1) * 128, f * slots : (f + 1) * slots] = (
-                sub == rank[f : f + 1]
+            send_place[d * room : (d + 1) * room, f * slots : (f + 1) * slots] = (
+                sub[:room] == rank[f : f + 1]
             ).astype(f32).astype(bf16)
     for f in range(FACES):
         at = slice(f * slots, (f + 1) * slots)
         contrib[width : width + 1, at] = goal_slot[f : f + 1].astype(f32)
         contrib[width + 1 : width + 2, at] = goal_face[f : f + 1].astype(f32) + 1.0
         contrib[width + 2 : pitch, at] = jnp.zeros((pitch - width - 2, slots), f32)
+    pl.semaphore_wait(barrier, owners - 1)
     face_row = jnp.concatenate([goal_face[f : f + 1] for f in range(FACES)], axis=1)
 
     def by_lane(row, index):
         return row[:, index : index + 1]
 
-    norm = by_lane(end_total(0, mine), 0) * scale
-    beta = jnp.sqrt(norm + 1e-06)
-    basis_ref[0] = start / beta
-    cross = {(0, 0): norm / (beta * beta)}
+    left = lax.broadcasted_iota(jnp.int32, (half, slots), 1) < room
+
+    def fold(wide):
+        top, low = wide[:half], wide[half:]
+        return (
+            jnp.where(left, top, pltpu.roll(low, room, 1)),
+            jnp.where(left, pltpu.roll(top, room, 1), low),
+        )
+
+    def unfold(one, two):
+        return jnp.concatenate(
+            [
+                jnp.where(left, one, pltpu.roll(two, room, 1)),
+                jnp.where(left, pltpu.roll(one, room, 1), two),
+            ],
+            axis=0,
+        )
+
+    def deliver(values, faces_at, place, shift):
+        placed = jnp.concatenate(
+            [jnp.where(faces_at == g + shift, values, 0.0) for g in range(FACES)], axis=0
+        ).astype(bf16)
+        at_faces = lax.dot_general(
+            placed, place, (((1,), (1,)), ((), ())), preferred_element_type=f32
+        )
+        return jnp.dot(spread_ref[...], at_faces.astype(bf16), preferred_element_type=f32)
+
+    cross = {}
     hess = {}
     arrived_place = None
+    whole = unknowns // 8
+    beta = None
+    shift = 1.0
+
+    def normalise(step, mine):
+        summed = end_total(step, mine) * scale
+        last = step - 1
+        heights = [by_lane(summed, i) for i in range(step)]
+        rest = images[last, :unknowns, :]
+        for i, h in enumerate(heights):
+            rest = rest - h * basis_ref[i]
+        along = [
+            heights[i]
+            - sum(heights[k] * cross[min(i, k), max(i, k)] for k in range(step))
+            for i in range(step)
+        ]
+        square = by_lane(summed, step) - sum(
+            heights[i] * (heights[i] + along[i]) for i in range(step)
+        )
+        square = jnp.maximum(square, 0.0)
+        height = jnp.sqrt(square + 1e-06)
+        inverse = 1.0 / height
+        basis_ref[step] = rest * inverse
+        for i in range(step):
+            hess[i, last] = heights[i]
+            cross[i, step] = along[i] * inverse
+        hess[step, last] = height
+        cross[step, step] = square * inverse * inverse
+        return heights, inverse
 
     for step in range(STEPS):
-        rounded = basis_ref[step].astype(bf16)
+        if step == 0:
+            source = start
+        else:
+            source = images[step - 1, :unknowns, :] - shift * basis_ref[step - 1]
+        rounded = source.astype(bf16)
         if step == 0:
             loads[0].wait()
 
@@ -177,7 +232,6 @@
             fields[step, at, :] = row_sums(precond[at], rounded, 128)
             return carry
 
-        whole = unknowns // 8
         lax.fori_loop(0, whole, precondition, 0)
         fields[step, whole * 8 : unknowns, :] = row_sums(
             precond[whole * 8 : unknowns], rounded, 128
@@ -192,12 +246,16 @@
             for k in range(0, width, 8):
                 top = min(k + 8, width)
                 contrib[k:top, at] = row_sums(face[f, k:top], vector, 32)
-        sent = contrib[...].astype(bf16)
         packed = lax.dot_general(
-            sent, send_place[...], (((1,), (1,)), ((), ())), preferred_element_type=f32
-        )
-        for d in range(len(OFFSETS)):
-            halo_out[step, d] = packed[:, d * 128 : (d + 1) * 128]
+            contrib[...].astype(bf16),
+            send_place[...],
+            (((1,), (1,)), ((), ())),
+            preferred_element_type=f32,
+        )
+        for d in range(0, len(OFFSETS), 2):
+            halo_out[step, d], halo_out[step, d + 1] = fold(
+                packed[:, d * room : (d + 2) * room]
+            )
         copies = []
         for d, offset in enumerate(OFFSETS):
             copies.append(
@@ -213,65 +271,66 @@
             copies[-1].start()
 
         if step == 0:
+            products = [start * start]
+        else:
+            newest = images[step - 1, :unknowns, :]
+            products = [basis_ref[i] * newest for i in range(step)] + [newest * newest]
+        mine = begin_total(step, [jnp.sum(x, axis=0, keepdims=True) for x in products])
+
+        if step == 0:
             loads[2].wait()
 
         def diagonal(b, carry):
             at = pl.ds(pl.multiple_of(b * 8, 8), 8)
-            image[at, :] = row_sums(diag[at], applied, 128)
+            images[step, at, :] = row_sums(diag[at], applied, 128)
             return carry
 
         lax.fori_loop(0, whole, diagonal, 0)
-        image[whole * 8 : unknowns, :] = row_sums(diag[whole * 8 : unknowns], applied, 128)
-
-        def deliver(values, faces_at, place, shift):
-            placed = jnp.concatenate(
-                [jnp.where(faces_at == g + shift, values, 0.0) for g in range(FACES)], axis=0
-            ).astype(bf16)
-            return lax.dot_general(
-                placed, place, (((1,), (1,)), ((), ())), preferred_element_type=f32
-            )
-
-        at_faces = deliver(contrib[...], face_row, local_place[...], 0)
+        images[step, whole * 8 : unknowns, :] = row_sums(
+            diag[whole * 8 : unknowns], applied, 128
+        )
+        total = images[step, :unknowns, :] + deliver(
+            contrib[...], face_row, local_place[...], 0
+        )
         for copy in copies:
             copy.wait_recv()
-        got = jnp.concatenate([halo_in[step, d] for d in range(len(OFFSETS))], axis=1)
+        got = jnp.concatenate(
+            [
+                unfold(halo_in[step, d], halo_in[step, d + 1])
+                for d in range(0, len(OFFSETS), 2)
+            ],
+            axis=1,
+        )
         got_slot = got[width : width + 1].astype(jnp.int32)
         got_face = got[width + 1 : width + 2].astype(jnp.int32)
         if step == 0:
             spots = lax.broadcasted_iota(jnp.int32, (slots, got.shape[1]), 0)
             arrived_place = (spots == got_slot).astype(f32).astype(bf16)
-        at_faces = at_faces + deliver(got, got_face, arrived_place, 1)
-        total = image[:unknowns, :] + jnp.dot(
-            spread_ref[...], at_faces.astype(bf16), preferred_element_type=f32
-        )
-        vectors = [basis_ref[i] for i in range(step + 1)]
-        mine = begin_total(
-            step + 1,
-            [jnp.sum(v * total, axis=0, keepdims=True) for v in vectors]
-            + [jnp.sum(total * total, axis=0, keepdims=True)],
-        )
-        summed = end_total(step + 1, mine) * scale
-        heights = [by_lane(summed, i) for i in range(step + 1)]
-        rest = total
-        for h, v in zip(heights, vectors):
-            rest = rest - h * v
-        along = [
-            heights[i]
-            - sum(heights[k] * cross[min(i, k), max(i, k)] for k in range(step + 1))
-            for i in range(step + 1)
-        ]
-        square = by_lane(summed, step + 1) - sum(
-            heights[i] * (heights[i] + along[i]) for i in range(step + 1)
-        )
-        square = jnp.maximum(square, 0.0)
-        height = jnp.sqrt(square + 1e-06)
-        inverse = 1.0 / height
-        basis_ref[step + 1] = rest * inverse
-        for i in range(step + 1):
-            hess[i, step] = heights[i]
-            cross[i, step + 1] = along[i] * inverse
-        hess[step + 1, step] = height
-        cross[step + 1, step + 1] = square * inverse * inverse
+        total = total + deliver(got, got_face, arrived_place, 1)
+        if step == 0:
+            norm = by_lane(end_total(0, mine), 0) * scale
+            beta = jnp.sqrt(norm + 1e-06)
+            inverse = 1.0 / beta
+            basis_ref[0] = start * inverse
+            cross[0, 0] = norm * inverse * inverse
+            images[0, :unknowns, :] = total * inverse
+            fields[0, :unknowns, :] = fields[0, :unknowns, :] * inverse
+        else:
+            heights, inverse = normalise(step, mine)
+            heights[step - 1] = heights[step - 1] - shift
+            field = fields[step, :unknowns, :]
+            for i in range(step):
+                total = total - heights[i] * images[i, :unknowns, :]
+                field = field - heights[i] * fields[i, :unknowns, :]
+            images[step, :unknowns, :] = total * inverse
+            fields[step, :unknowns, :] = field * inverse
+            shift = hess[step - 1, step - 1]
+
+    newest = images[STEPS - 1, :unknowns, :]
+    products = [basis_ref[i] * newest for i in range(STEPS)] + [newest * newest]
+    normalise(
+        STEPS, begin_total(STEPS, [jnp.sum(x, axis=0, keepdims=True) for x in products])
+    )
 
     rows = lax.broadcasted_iota(jnp.int32, hess_ref.shape, 0)
     cols = lax.broadcasted_iota(jnp.int32, hess_ref.shape, 1)
@@ -320,7 +379,7 @@
     width = face_blocks.shape[1]
     owners = lax.axis_size("dev")
     variables = unknowns // NODES
-    pitch = (width + 2 + 7) // 8 * 8
+    pitch = (width + 2 + 15) // 16 * 16
     padded = (unknowns + 7) // 8 * 8
     table = spread_table(variables, pitch)
     spread = jnp.asarray(table, jnp.bfloat16)
@@ -344,13 +403,13 @@
             pltpu.VMEM(diag_blocks.shape, bf16),
             pltpu.VMEM(precond.shape, bf16),
             pltpu.VMEM(face_blocks.shape, bf16),
-            pltpu.VMEM((padded, slots), f32),
+            pltpu.VMEM((STEPS, padded, slots), f32),
             pltpu.VMEM((STEPS, padded, slots), f32),
             pltpu.VMEM((pitch, FACES * slots), f32),
             pltpu.VMEM((slots, FACES * slots), bf16),
-            pltpu.VMEM((sides * 128, FACES * slots), bf16),
-            pltpu.VMEM((STEPS, sides, pitch, 128), f32),
-            pltpu.VMEM((STEPS, sides, pitch, 128), f32),
+            pltpu.VMEM((sides * (slots // 2), FACES * slots), bf16),
+            pltpu.VMEM((STEPS, sides, pitch // 2, slots), f32),
+            pltpu.VMEM((STEPS, sides, pitch // 2, slots), f32),
             pltpu.VMEM((STEPS + 1, 1, 128), f32),
             pltpu.VMEM((STEPS + 1, owners - 1, 1, 128), f32),
             dma((3,)),

time: 70 us -> 51.4 us (0.73)
  Pallas kernels: 63.9 us -> 45.3 us
    pallas_call x1, Pallas kernels: 63.9 us -> 45.3 us  [per_device(): pl.pallas_call(functools.partial(kernel, owners), out_shape=(jax.ShapeDty...]
where the time goes in v2:
time: 51.4 us; the launch traced here: 51.1 us
  Pallas kernels  45.3 us (88%)
  local copies, waits for them, and re-layouts  4.58 us (9%)
  between operations  1.29 us (3%)
    pallas_call x1, Pallas kernels, per_device(): pl.pallas_call(functools.partial(kernel, owners), out_shape=(jax.ShapeDty...  45.3 us
    unnamed x2, local copies, waits for them, and re-layouts  3.25 us
    pallas_call x1, local copies, waits for them, and re-layouts, per_device(): pl.pallas_call(functools.partial(kernel, owners), out_shape=(jax.ShapeDty...  1.33 us

profile of v2, /device:TPU:0, one launch (start us, length us, event | category | flops | bytes accessed | tf_op | source)
XLA Modules:
  0.0 51.1 jit_solution(3914147077605491789)
XLA Ops:
  1.3 45.3 %shard_map.112 = (f32[5,135,128]{2,1,0:T(8,128)}, f32[5,4]{1,0:T(8,128)}, f32[135,128]{1,0:T(8,128)}) custom-call(s32[1]{0:T(128)S(6)} %copy.15.live_ref, f32[135,128]{1,0:T(8,128)} %rhs_ref.1, s32[6,128]{1,0:T(8,128)} %nbr_elem_ref.1, s32[6,128]{1,0:T(8,128)} %nbr_face_ref.1, bf16[135,288]{1,0:T(8,128)(2,1)} %constant.4.clone.spread_ref, ...), custom_call_target="tpu_custom_call" | custom-call | tf_op jit(solution)/shard_map/pallas_call | solution.py:393
  46.6 1.3 %copy.12 = f32[5,4]{0,1:T(4,128)} copy(f32[5,4]{1,0:T(8,128)} %get-tuple-element.4) | data formatting | bytes 160 | tf_op jit(solution)/shard_map/pallas_call | solution.py:393
  47.9 1.7 %copy.16 = f32[5,135,128]{2,1,0:T(8,128)} copy(f32[5,135,128]{2,1,0:T(8,128)} %get-tuple-element.9) | data formatting | bytes 691200
  49.6 1.5 %copy.17 = f32[135,128]{1,0:T(8,128)} copy(f32[135,128]{1,0:T(8,128)} %get-tuple-element.11) | data formatting | bytes 138240

commit v3 on v2

--- a/solution.py
+++ b/solution.py
@@ -38,39 +38,68 @@
     return table
 
 
-def row_sums(block, vector, split):
-    half = split // 2
-    head = block[:, :half] * vector[None, :half] + block[:, half:split] * vector[None, half:split]
-    tail = block[:, split:] * vector[None, split:]
-    both = jnp.concatenate([head.astype(jnp.float32), tail.astype(jnp.float32)], axis=1)
-    return jnp.sum(both, axis=1)
+def row_sums(main, tail, lead, first, count, vector, rest):
+    f32 = jnp.float32
+    height, double = main.shape[-2:]
+    lanes = double // 2
+    tiles = height // 8
+    sums = []
+    for r in range(count):
+        at = lead + (first + r,)
+        products = [
+            main[at + (slice(c * 8, c * 8 + 8),)] * vector[c * 8 : c * 8 + 8]
+            for c in range(tiles)
+        ]
+        pairs = [(products[c] + products[c + 1]).astype(f32) for c in range(0, tiles, 2)]
+        parts = [p[:, :lanes] for p in pairs] + [p[:, lanes:] for p in pairs]
+        parts.append((tail[at] * rest).astype(f32))
+        sums.append(jnp.sum(jnp.concatenate(parts, axis=0), axis=0, keepdims=True))
+    return jnp.concatenate(sums, axis=0)
 
 
 def kernel(
     owners, live_ref, rhs_ref, nbr_elem_ref, nbr_face_ref, spread_ref, trace_ref,
     diag_hbm, precond_hbm, face_hbm,
     basis_ref, hess_ref, update_ref,
-    diag, precond, face, images, fields, contrib, local_place, send_place,
+    diag, diag_tail, precond, precond_tail, face, face_tail, images, fields, contrib, local_place, send_place,
     halo_out, halo_in, dots_out, dots_in,
     load_sems, halo_send, halo_recv, dots_send, dots_recv,
 ):
     f32, bf16 = jnp.float32, jnp.bfloat16
     unknowns, slots = rhs_ref.shape
-    width = face.shape[1]
+    width = face_hbm.shape[1]
     pitch = contrib.shape[0]
     room = slots // 2
     half = pitch // 2
     me = lax.axis_index("dev")
     scale = 1.0 / float(owners * slots * unknowns)
 
-    loads = [
-        pltpu.make_async_copy(src, dst, load_sems.at[k])
-        for k, (src, dst) in enumerate(
-            [(precond_hbm, precond), (face_hbm, face), (diag_hbm, diag)]
-        )
-    ]
-    for load in loads:
-        load.start()
+    loads = []
+    for k, (src, main, tail) in enumerate(
+        ((precond_hbm, precond, precond_tail), (face_hbm, face, face_tail), (diag_hbm, diag, diag_tail))
+    ):
+        height, inputs = main.shape[-2], src.shape[-2]
+        lead = (slice(None),) * (len(main.shape) - 2)
+        pieces = [
+            (src.at[lead + (pl.ds(0, height),)], main.at[lead + (slice(None), pl.ds(0, slots))]),
+            (
+                src.at[lead + (pl.ds(height, height),)],
+                main.at[lead + (slice(None), pl.ds(slots, slots))],
+            ),
+            (src.at[lead + (pl.ds(2 * height, inputs - 2 * height),)], tail),
+        ]
+        loads.append(
+            [
+                pltpu.make_async_copy(*piece, load_sems.at[3 * k + m])
+                for m, piece in enumerate(pieces)
+            ]
+        )
+        for piece in loads[-1]:
+            piece.start()
+
+    def loaded(k):
+        for piece in loads[k]:
+            piece.wait()
 
     barrier = pltpu.get_barrier_semaphore()
 
@@ -185,6 +214,10 @@
         )
         return jnp.dot(spread_ref[...], at_faces.astype(bf16), preferred_element_type=f32)
 
+    def beside(column, height):
+        both = jnp.concatenate([column[:height], column[height : 2 * height]], axis=1)
+        return both.astype(bf16), column[2 * height :].astype(bf16)
+
     cross = {}
     hess = {}
     arrived_place = None
@@ -223,29 +256,32 @@
             source = start
         else:
             source = images[step - 1, :unknowns, :] - shift * basis_ref[step - 1]
-        rounded = source.astype(bf16)
-        if step == 0:
-            loads[0].wait()
+        rounded, rounded_tail = beside(source, precond.shape[-2])
+        if step == 0:
+            loaded(0)
 
         def precondition(b, carry):
             at = pl.ds(pl.multiple_of(b * 8, 8), 8)
-            fields[step, at, :] = row_sums(precond[at], rounded, 128)
+            fields[step, at, :] = row_sums(precond, precond_tail, (), b * 8, 8, rounded, rounded_tail)
             return carry
 
         lax.fori_loop(0, whole, precondition, 0)
         fields[step, whole * 8 : unknowns, :] = row_sums(
-            precond[whole * 8 : unknowns], rounded, 128
+            precond, precond_tail, (), whole * 8, unknowns - whole * 8, rounded, rounded_tail
         )
         applied = fields[step, :unknowns, :].astype(bf16)
-        traced = jnp.dot(trace_ref[...], applied, preferred_element_type=f32).astype(bf16)
-        if step == 0:
-            loads[1].wait()
+        halves, halves_tail = beside(fields[step, :unknowns, :], diag.shape[-2])
+        traced = jnp.dot(trace_ref[...], applied, preferred_element_type=f32)
+        if step == 0:
+            loaded(1)
         for f in range(FACES):
-            vector = traced[f * pitch : f * pitch + width]
+            vector, rest = beside(traced[f * pitch : f * pitch + width], face.shape[-2])
             at = slice(f * slots, (f + 1) * slots)
             for k in range(0, width, 8):
                 top = min(k + 8, width)
-                contrib[k:top, at] = row_sums(face[f, k:top], vector, 32)
+                contrib[k:top, at] = row_sums(
+                    face, face_tail, (f,), k, top - k, vector, rest
+                )
         packed = lax.dot_general(
             contrib[...].astype(bf16),
             send_place[...],
@@ -278,16 +314,16 @@
         mine = begin_total(step, [jnp.sum(x, axis=0, keepdims=True) for x in products])
 
         if step == 0:
-            loads[2].wait()
+            loaded(2)
 
         def diagonal(b, carry):
             at = pl.ds(pl.multiple_of(b * 8, 8), 8)
-            images[step, at, :] = row_sums(diag[at], applied, 128)
+            images[step, at, :] = row_sums(diag, diag_tail, (), b * 8, 8, halves, halves_tail)
             return carry
 
         lax.fori_loop(0, whole, diagonal, 0)
         images[step, whole * 8 : unknowns, :] = row_sums(
-            diag[whole * 8 : unknowns], applied, 128
+            diag, diag_tail, (), whole * 8, unknowns - whole * 8, halves, halves_tail
         )
         total = images[step, :unknowns, :] + deliver(
             contrib[...], face_row, local_place[...], 0
@@ -332,8 +368,8 @@
         STEPS, begin_total(STEPS, [jnp.sum(x, axis=0, keepdims=True) for x in products])
     )
 
-    rows = lax.broadcasted_iota(jnp.int32, hess_ref.shape, 0)
-    cols = lax.broadcasted_iota(jnp.int32, hess_ref.shape, 1)
+    cols = lax.broadcasted_iota(jnp.int32, hess_ref.shape, 0)
+    rows = lax.broadcasted_iota(jnp.int32, hess_ref.shape, 1)
     table = jnp.zeros(hess_ref.shape, f32)
     for (i, j), value in hess.items():
         table = jnp.where((rows == i) & (cols == j), value, table)
@@ -387,22 +423,31 @@
     f32, bf16 = jnp.float32, jnp.bfloat16
     vmem = pl.BlockSpec(memory_space=pltpu.VMEM)
     smem = pl.BlockSpec(memory_space=pltpu.SMEM)
-    hbm = pl.BlockSpec(memory_space=pl.ANY)
+    hbm = pl.BlockSpec(memory_space=pltpu.HBM)
     sides = len(OFFSETS)
     dma = pltpu.SemaphoreType.DMA
-    return pl.pallas_call(
+
+    def halves(block):
+        lead, inputs = block.shape[:-2], block.shape[-2]
+        split = inputs // 32 * 16
+        return [
+            pltpu.VMEM(lead + (split, 2 * slots), bf16),
+            pltpu.VMEM(lead + (inputs - 2 * split, slots), bf16),
+        ]
+
+    basis, hess, update = pl.pallas_call(
         functools.partial(kernel, owners),
         out_shape=(
             jax.ShapeDtypeStruct((STEPS + 1, unknowns, slots), f32),
-            jax.ShapeDtypeStruct((STEPS + 1, STEPS), f32),
+            jax.ShapeDtypeStruct((STEPS, STEPS + 1), f32),
             jax.ShapeDtypeStruct((unknowns, slots), f32),
         ),
         in_specs=[smem, vmem, vmem, vmem, vmem, vmem, hbm, hbm, hbm],
         out_specs=(vmem, vmem, vmem),
         scratch_shapes=[
-            pltpu.VMEM(diag_blocks.shape, bf16),
-            pltpu.VMEM(precond.shape, bf16),
-            pltpu.VMEM(face_blocks.shape, bf16),
+            *halves(diag_blocks),
+            *halves(precond),
+            *halves(face_blocks),
             pltpu.VMEM((STEPS, padded, slots), f32),
             pltpu.VMEM((STEPS, padded, slots), f32),
             pltpu.VMEM((pitch, FACES * slots), f32),
@@ -412,16 +457,17 @@
             pltpu.VMEM((STEPS, sides, pitch // 2, slots), f32),
             pltpu.VMEM((STEPS + 1, 1, 128), f32),
             pltpu.VMEM((STEPS + 1, owners - 1, 1, 128), f32),
-            dma((3,)),
+            dma((9,)),
             dma((STEPS, sides)),
             dma((STEPS, sides)),
             dma((STEPS + 1,)),
             dma((STEPS + 1,)),
         ],
         compiler_params=pltpu.CompilerParams(
-            collective_id=0, has_side_effects=True, vmem_limit_bytes=56 * 1024 * 1024
+            collective_id=0, has_side_effects=True, vmem_limit_bytes=52 * 1024 * 1024
         ),
     )(live, rhs, nbr_elem, nbr_face, spread, trace, diag_blocks, precond, face_blocks)
+    return basis, hess.T, update
 
 
 def solution(mesh):

time: 51.4 us -> 48.7 us (0.947)
  Pallas kernels: 45.3 us -> 41.2 us
  local copies, waits for them, and re-layouts: 4.58 us -> 6 us
    pallas_call x1, Pallas kernels: 45.3 us -> 41.2 us  [per_device(): pl.pallas_call(functools.partial(kernel, owners), out_shape=(jax.ShapeDty...]
    unnamed x2 -> x13, local copies, waits for them, and re-layouts: 3.25 us -> 6 us
    pallas_call x1 -> x0, local copies, waits for them, and re-layouts: 1.33 us -> none  [per_device(): pl.pallas_call(functools.partial(kernel, owners), out_shape=(jax.ShapeDty...]
where the time goes in v3:
time: 48.7 us; the launch traced here: 48.5 us
  Pallas kernels  41.2 us (85%)
  local copies, waits for them, and re-layouts  6 us (12%)
  between operations  1.3 us (3%)
    pallas_call x1, Pallas kernels, per_device(): pl.pallas_call(functools.partial(kernel, owners), out_shape=(jax.ShapeDty...  41.2 us
    unnamed x13, local copies, waits for them, and re-layouts  6 us

profile of v3, /device:TPU:0, one launch (start us, length us, event | category | flops | bytes accessed | tf_op | source)
XLA Modules:
  0.0 48.5 jit_solution(6708973205546792913)
XLA Ops:
  1.3 0.0 copy-start
  1.3 0.9 %copy-done = bf16[288,135]{1,0:T(8,128)(2,1)S(1)} copy-done((bf16[288,135]{1,0:T(8,128)(2,1)S(1)}, bf16[288,135]{1,0:T(8,128)(2,1)}, u32[]{:S(2)}) %copy-start) | copy-done | bytes 77784
  2.2 0.0 copy-start.1
  2.2 0.9 %copy-done.1 = bf16[135,288]{1,0:T(8,128)(2,1)S(1)} copy-done((bf16[135,288]{1,0:T(8,128)(2,1)S(1)}, bf16[135,288]{1,0:T(8,128)(2,1)}, u32[]{:S(2)}) %copy-start.1) | copy-done | bytes 77784
  3.1 0.0 copy-start.2
  3.1 0.9 %copy-done.2 = f32[135,128]{1,0:T(8,128)S(1)} copy-done((f32[135,128]{1,0:T(8,128)S(1)}, f32[135,128]{1,0:T(8,128)}, u32[]{:S(2)}) %copy-start.2) | copy-done | bytes 69144
  4.0 0.0 copy-start.3
  4.0 0.7 %copy-done.3 = s32[6,128]{1,0:T(8,128)S(1)} copy-done((s32[6,128]{1,0:T(8,128)S(1)}, s32[6,128]{1,0:T(8,128)}, u32[]{:S(2)}) %copy-start.3) | copy-done | bytes 3096
  4.7 0.0 copy-start.4
  4.7 0.7 %copy-done.4 = s32[6,128]{1,0:T(8,128)S(1)} copy-done((s32[6,128]{1,0:T(8,128)S(1)}, s32[6,128]{1,0:T(8,128)}, u32[]{:S(2)}) %copy-start.4) | copy-done | bytes 3096
  5.3 41.2 %shard_map.112 = (f32[5,135,128]{2,1,0:T(8,128)S(1)}, f32[4,5]{1,0:T(4,128)S(1)}, f32[135,128]{1,0:T(8,128)S(1)}) custom-call(s32[1]{0:T(128)S(6)} %copy.15.live_ref, f32[135,128]{1,0:T(8,128)S(1)} %copy-done.2, s32[6,128]{1,0:T(8,128)S(1)} %copy-done.3, s32[6,128]{1,0:T(8,128)S(1)} %copy-done.4, bf16[135,288]{1,0:T(8,128)(2,1)S(1)} %copy-done.1, ...), custom_call_target="tpu_custom_call" | custom-call | tf_op jit(solution)/shard_map/pallas_call | solution.py:438
  46.5 0.7 %copy.16 = f32[5,135,128]{2,1,0:T(8,128)} copy(f32[5,135,128]{2,1,0:T(8,128)S(1)} %get-tuple-element.12) | data formatting | bytes 691200
  47.2 0.6 %copy.17 = f32[5,4]{0,1:T(4,128)} copy(f32[5,4]{0,1:T(4,128)S(1)} %bitcast.1) | data formatting | bytes 160
  47.8 0.6 %copy.18 = f32[135,128]{1,0:T(8,128)} copy(f32[135,128]{1,0:T(8,128)S(1)} %get-tuple-element.14) | data formatting | bytes 138240
Async XLA Ops:
  1.3 0.9 %copy-start = (bf16[288,135]{1,0:T(8,128)(2,1)S(1)}, bf16[288,135]{1,0:T(8,128)(2,1)}, u32[]{:S(2)}) copy-start(bf16[288,135]{1,0:T(8,128)(2,1)} %constant.5.clone.trace_ref) | copy-start | bytes 233284
  2.2 0.9 %copy-start.1 = (bf16[135,288]{1,0:T(8,128)(2,1)S(1)}, bf16[135,288]{1,0:T(8,128)(2,1)}, u32[]{:S(2)}) copy-start(bf16[135,288]{1,0:T(8,128)(2,1)} %constant.4.clone.spread_ref) | copy-start | bytes 233284
  3.1 0.9 %copy-start.2 = (f32[135,128]{1,0:T(8,128)S(1)}, f32[135,128]{1,0:T(8,128)}, u32[]{:S(2)}) copy-start(f32[135,128]{1,0:T(8,128)} %rhs_ref.1) | copy-start | bytes 207364
  4.0 0.7 %copy-start.3 = (s32[6,128]{1,0:T(8,128)S(1)}, s32[6,128]{1,0:T(8,128)}, u32[]{:S(2)}) copy-start(s32[6,128]{1,0:T(8,128)} %nbr_elem_ref.1) | copy-start | bytes 9220
  4.7 0.7 %copy-start.4 = (s32[6,128]{1,0:T(8,128)S(1)}, s32[6,128]{1,0:T(8,128)}, u32[]{:S(2)}) copy-start(s32[6,128]{1,0:T(8,128)} %nbr_face_ref.1) | copy-start | bytes 9220

commit v4 on v3

--- a/solution.py
+++ b/solution.py
@@ -408,6 +408,12 @@
     for round_id in range(STEPS + 1):
         arrived = dots_in.at[round_id]
         pltpu.make_async_copy(arrived, arrived, dots_send.at[round_id]).wait()
+
+
+def hand_over(*refs):
+    half = len(refs) // 2
+    for source, target in zip(refs[:half], refs[half:]):
+        target[...] = source[...]
 
 
 def per_device(rhs, diag_blocks, precond, face_blocks, nbr_elem, nbr_face, live):
@@ -464,9 +470,16 @@
             dma((STEPS + 1,)),
         ],
         compiler_params=pltpu.CompilerParams(
-            collective_id=0, has_side_effects=True, vmem_limit_bytes=52 * 1024 * 1024
+            collective_id=0, has_side_effects=True, vmem_limit_bytes=60 * 1024 * 1024
         ),
     )(live, rhs, nbr_elem, nbr_face, spread, trace, diag_blocks, precond, face_blocks)
+    results = (basis, hess, update)
+    basis, hess, update = pl.pallas_call(
+        hand_over,
+        out_shape=[jax.ShapeDtypeStruct(r.shape, r.dtype) for r in results],
+        in_specs=[vmem] * 3,
+        out_specs=[vmem] * 3,
+    )(*results)
     return basis, hess.T, update
 
 

time: 48.7 us -> 46.2 us (0.949)
  local copies, waits for them, and re-layouts: 6 us -> 0 us
  Pallas kernels: 41.2 us -> 44.7 us
    unnamed x13 -> x0, local copies, waits for them, and re-layouts: 6 us -> none
    pallas_call x1, Pallas kernels: 41.2 us -> 42.9 us  [per_device(): pl.pallas_call(functools.partial(kernel, owners), out_shape=(jax.ShapeDty...]
    pallas_call x0 -> x1, Pallas kernels: none -> 1.76 us  [per_device(): pl.pallas_call(hand_over, out_shape=[jax.ShapeDtypeStruct(r.shape, r.dtyp...]
where the time goes in v4:
time: 46.2 us; the launch traced here: 46 us
  Pallas kernels  44.7 us (97%)
  between operations  1.29 us (3%)
    pallas_call x1, Pallas kernels, per_device(): pl.pallas_call(functools.partial(kernel, owners), out_shape=(jax.ShapeDty...  42.9 us
    pallas_call x1, Pallas kernels, per_device(): pl.pallas_call(hand_over, out_shape=[jax.ShapeDtypeStruct(r.shape, r.dtyp...  1.76 us

profile of v4, /device:TPU:0, one launch (start us, length us, event | category | flops | bytes accessed | tf_op | source)
XLA Modules:
  0.0 46.0 jit_solution(3660017450659951885)
XLA Ops:
  1.3 42.9 %shard_map.112 = (f32[5,135,128]{2,1,0:T(8,128)}, f32[4,5]{1,0:T(4,128)}, f32[135,128]{1,0:T(8,128)}) custom-call(s32[1]{0:T(128)S(6)} %copy.12.live_ref, f32[135,128]{1,0:T(8,128)} %rhs_ref.1, s32[6,128]{1,0:T(8,128)} %nbr_elem_ref.1, s32[6,128]{1,0:T(8,128)} %nbr_face_ref.1, bf16[135,288]{1,0:T(8,128)(2,1)} %constant.4.clone.spread_ref, ...), custom_call_target="tpu_custom_call" | custom-call | tf_op jit(solution)/shard_map/pallas_call | solution.py:444
  44.2 1.8 %shard_map.113 = (f32[5,135,128]{2,1,0:T(8,128)}, f32[4,5]{1,0:T(4,128)}, f32[135,128]{1,0:T(8,128)}) custom-call(f32[5,135,128]{2,1,0:T(8,128)} %get-tuple-element.9.refs_0_, f32[4,5]{1,0:T(4,128)} %get-tuple-element.10.refs_1_, f32[135,128]{1,0:T(8,128)} %get-tuple-element.11.refs_2_), custom_call_target="tpu_custom_call" | custom-call | tf_op jit(solution)/shard_map/pallas_call | solution.py:477
